TPU v7x, 512 devices: a whole 4x4x16 slice. The times are simulated.
512 devices in a mesh: tp: 16 (over z_hi, y, core), dp: 32 (over z_lo, x).
Axes of the slice: x: 4, y: 4, z: 16 (z_hi: 2, z_lo: 8; z = z_hi * 8 + z_lo), core: 2. Of those that a mesh axis runs over, the one named last changes fastest.
Arguments:
- tokens: bfloat16 [2048, 4096], P(('tp', 'dp')), may hold values from -6 to 6
- norm_gain: float32 [4096], replicated, may hold values from 0.1 to 1.9
- gate_slots: bfloat16 [1536, 128, 128], P(('tp', 'dp')), may hold values from -0.1875 to 0.1875
- up_slots: bfloat16 [1536, 128, 128], P(('tp', 'dp')), may hold values from -0.1875 to 0.1875
- down_slots: bfloat16 [1536, 128, 128], P(('tp', 'dp')), may hold values from -0.09375 to 0.09375
- gate_ids: int32 [1536], P('tp'), may hold values from -1 to 223, as said below
- up_ids: int32 [1536], P('tp'), may hold values from -1 to 223, as said below
- down_ids: int32 [1536], P('tp'), may hold values from -1 to 223, as said below
Outputs:
- mixed: bfloat16 [2048, 4096], P(('tp', 'dp'))
Inputs may be any that keep to these rules, and one draw needn't show every extreme that they name: `gate_ids`: each entry is -1 (an empty slot) or a block number j * 32 + k, j a hidden block of that tp index and k a block of the model width. The live numbers of one tp index are distinct and stand in its first slots; each tp index keeps at most 96 blocks, and one tp index keeps exactly 96. `up_ids`: as for gate_ids, drawn independently. `down_ids`: as for gate_ids, drawn independently.
All inputs are finite; a program needn't handle non-finite values.
Results may differ from a plain program's by a relative error of at most 0.015.
Values may be sent and summed in bfloat16 or wider, within the bound.
A program may use at most 128 MiB of HBM per device.

v0:
```python
import jax
import jax.numpy as jnp
from jax import lax
from jax.sharding import PartitionSpec as P

FF = 14336


EPSILON = 1e-05


def normalize(tokens, norm_gain):
    values = tokens.astype(jnp.float32)
    meansq = jnp.mean(values * values, axis=-1, keepdims=True)
    return (values * lax.rsqrt(meansq + EPSILON) * norm_gain).astype(jnp.bfloat16)


def decode(slot_ids, kblocks):
    slot_live = slot_ids >= 0
    hidden_block = jnp.where(slot_live, slot_ids // kblocks, 0)
    depth_block = jnp.where(slot_live, slot_ids % kblocks, 0)
    return (hidden_block, depth_block, slot_live)


def block_terms(inputs, slot_values, source, target, slot_live, width_in, width_out):
    block_side = slot_values.shape[1]
    rows_count = inputs.shape[0]
    blocked = inputs.reshape(rows_count, width_in, block_side)
    picked = jnp.take(blocked, source, axis=1)
    products = jnp.einsum("rca,cab->rcb", picked, slot_values, preferred_element_type=jnp.float32)
    placing = ((target[:, None] == jnp.arange(width_out)[None, :]) & slot_live[:, None]).astype(
        jnp.bfloat16
    )
    upper = products.astype(jnp.bfloat16)
    lower = (products - upper.astype(jnp.float32)).astype(jnp.bfloat16)
    summed = jnp.einsum("rcb,cn->rnb", upper, placing, preferred_element_type=jnp.float32)
    summed = summed + jnp.einsum("rcb,cn->rnb", lower, placing, preferred_element_type=jnp.float32)
    return summed.reshape(rows_count, width_out * block_side)


def shards(tokens, norm_gain, gate_slots, up_slots, down_slots, gate_ids, up_ids, down_ids):
    block_side = gate_slots.shape[1]
    model_width = tokens.shape[1]
    kblocks = model_width // block_side
    hblocks = FF // (block_side * lax.axis_size("tp"))
    normed = normalize(tokens, norm_gain)
    gathered = lax.all_gather(normed, "tp", axis=0, tiled=True)
    gate_hidden, gate_depth, gate_live = decode(gate_ids, kblocks)
    up_hidden, up_depth, up_live = decode(up_ids, kblocks)
    down_hidden, down_depth, down_live = decode(down_ids, kblocks)
    all_gate, all_up, all_down = (
        lax.all_gather(gate_slots, "dp", axis=0, tiled=True),
        lax.all_gather(up_slots, "dp", axis=0, tiled=True),
        lax.all_gather(down_slots, "dp", axis=0, tiled=True),
    )
    gate_act = block_terms(gathered, all_gate, gate_depth, gate_hidden, gate_live, kblocks, hblocks)
    up_act = block_terms(gathered, all_up, up_depth, up_hidden, up_live, kblocks, hblocks)
    hidden = (jax.nn.silu(gate_act) * up_act).astype(jnp.bfloat16)
    partial_value = block_terms(
        hidden, all_down, down_hidden, down_depth, down_live, hblocks, kblocks
    )
    branch_sum = lax.psum_scatter(
        partial_value.astype(jnp.bfloat16), "tp", scatter_dimension=0, tiled=True
    ).astype(jnp.float32)
    return (tokens.astype(jnp.float32) + branch_sum).astype(jnp.bfloat16)


def solution(mesh):
    placed = (
        P(("tp", "dp"), None),
        P(),
        P(("tp", "dp"), None, None),
        P(("tp", "dp"), None, None),
        P(("tp", "dp"), None, None),
        P("tp"),
        P("tp"),
        P("tp"),
    )
    return jax.shard_map(
        shards, mesh=mesh, in_specs=placed, out_specs=P(("tp", "dp"), None), check_vma=False
    )
```

profile of v0, /device:TPU:1, one launch (start us, length us, event | category | flops | bytes accessed | tf_op | source)
XLA Modules:
  0.0 964.0 jit_solution(2715450965105830085)
XLA Ops:
  6.5 0.7 all-gather.5.cloned.1.call-update
  7.3 0.0 all-gather.7.cloned.1.call-start
  7.3 0.7 all-gather.7.cloned.1.call-update
  8.0 0.0 all-gather.9.cloned.1.call-start
  8.1 0.7 all-gather.9.cloned.1.call-update
  8.7 0.0 all-reduce.3.cloned.1.call-start
  8.8 0.9 fusion.54
  9.7 0.9 fusion.58
  10.6 55.3 %all-gather = bf16[16,4,4096]{2,1,0:T(4,128)(2,1)S(1)} all-gather(bf16[1,4,4096]{2,1,0:T(4,128)(2,1)S(1)} %fusion.58), channel_id=1, replica_groups=mesh['tp'=16,'dp'=32] {'tp'}, dimensions={0}, use_global_device_ids=true | all-gather | bytes 557056 | tf_op jit(solution)/shard_map/all_gather | solution.py:47
  65.8 0.5 reshape.34
  66.4 0.2 copy.28
  66.6 0.0 copy-start.2
  66.6 1.9 gather_fusion.1
  68.6 0.8 gather_fusion.2
  69.6 152.0 %all-gather.5.cloned.1.call-done = bf16[96,128,128]{2,1,0:T(8,128)(2,1)} async-done(((bf16[3,128,128]{2,1,0:T(8,128)(2,1)}), bf16[96,128,128]{2,1,0:T(8,128)(2,1)}) %all-gather.5.cloned.1.call-update) | async-done | bytes 3145744 | tf_op jit(solution)/shard_map/all_gather | solution.py:52
  221.5 3.4 fusion.2
  224.9 0.9 fusion.17
  225.8 222.5 %all-gather.7.cloned.1.call-done = bf16[96,128,128]{2,1,0:T(8,128)(2,1)} async-done(((bf16[3,128,128]{2,1,0:T(8,128)(2,1)}), bf16[96,128,128]{2,1,0:T(8,128)(2,1)}) %all-gather.7.cloned.1.call-update) | async-done | bytes 3145744 | tf_op jit(solution)/shard_map/all_gather | solution.py:53
  448.3 2.9 fusion.1
  451.2 0.9 fusion.13
  452.2 0.9 fusion.36
  453.1 1.0 fusion.48
  454.1 0.8 gather_fusion
  455.0 219.7 %all-gather.9.cloned.1.call-done = bf16[96,128,128]{2,1,0:T(8,128)(2,1)} async-done(((bf16[3,128,128]{2,1,0:T(8,128)(2,1)}), bf16[96,128,128]{2,1,0:T(8,128)(2,1)}) %all-gather.9.cloned.1.call-update) | async-done | bytes 3145744 | tf_op jit(solution)/shard_map/all_gather | solution.py:54
  674.7 2.9 fusion
  677.6 1.0 fusion.9
  678.6 1.1 fusion.30
  679.7 1.0 copy.67
  680.7 0.0 all-reduce.3.cloned.1.call-update
  680.8 1.3 dynamic-slice
  682.7 273.2 %all-reduce.3.cloned.1.call-done = bf16[64,4096]{1,0:T(8,128)(2,1)} async-done(((bf16[64,4096]{1,0:T(8,128)(2,1)}), bf16[64,4096]{1,0:T(8,128)(2,1)}) %all-reduce.3.cloned.1.call-update) | async-done | bytes 524304
  955.9 1.5 fusion.57
  (19 shorter events, 0.1 us)
Async XLA Ops:
  6.5 60.1 %copy-start.1 = (s32[96]{0:T(128)S(1)}, s32[96]{0:T(128)}, u32[]{:S(2)}) copy-start(s32[96]{0:T(128)} %param.15) | copy-start | bytes 1156
  6.5 215.0 %all-gather.5.cloned.1.call-start = ((), (), s32[]{:S(2)}) async-start(), calls=%async_computation | async-start | bytes 3244032 | tf_op jit(solution)/shard_map/all_gather | solution.py:52
  7.3 441.1 %all-gather.7.cloned.1.call-start = ((), (), s32[]{:S(2)}) async-start(), calls=%async_computation.1 | async-start | bytes 3244032 | tf_op jit(solution)/shard_map/all_gather | solution.py:53
  8.0 666.7 %all-gather.9.cloned.1.call-start = ((), (), s32[]{:S(2)}) async-start(), calls=%async_computation.2 | async-start | bytes 3244032 | tf_op jit(solution)/shard_map/all_gather | solution.py:54
  8.7 947.2 %all-reduce.3.cloned.1.call-start = ((), (), s32[]{:S(2)}) async-start(), calls=%async_computation.3 | async-start | bytes 1048576
  66.6 2.0 copy-start.2
  68.6 0.9 copy-start.3
  679.7 276.2 %copy-start = (bf16[4,4096]{1,0:T(4,128)(2,1)S(1)}, bf16[4,4096]{1,0:T(4,128)(2,1)}, u32[]{:S(2)}) copy-start(bf16[4,4096]{1,0:T(4,128)(2,1)} %param.10) | copy-start | bytes 98308
Sparse Core Ops, SparseCore 0:
  9.4 212.0 all-gather.4
  223.6 224.6 all-gather.6
  450.4 224.2 all-gather.8
  680.9 275.0 all-reduce.2
where the time goes:
time: 964 us
  waiting for transfers between devices  869 us (90%)
  blocking collectives  55.3 us (6%)
  matrix products  15.1 us (2%)
  between operations  13.9 us (1%)
    unnamed x5, waiting for transfers between devices  275 us
    all_gather x1, waiting for transfers between devices, shards(): lax.all_gather(up_slots, 'dp', axis=0, tiled=True)  222 us
    all_gather x1, waiting for transfers between devices, shards(): lax.all_gather(down_slots, 'dp', axis=0, tiled=True)  220 us
    all_gather x1, waiting for transfers between devices, shards(): lax.all_gather(gate_slots, 'dp', axis=0, tiled=True)  152 us
    all_gather x1, blocking collectives, shards(): gathered = lax.all_gather(normed, 'tp', axis=0, tiled=True)  55.3 us
  transfers between devices with their start and end apart: 4, of which 4 were waited for; matrix products, arithmetic and copies ran while one was open for 2% of the time, Pallas kernels for 0%

commit v1 on v0

v1 whole, which is shorter than its diff:
```python
import jax
import jax.numpy as jnp
from jax import lax
from jax.experimental import pallas as pl
from jax.experimental.pallas import tpu as pltpu
from jax.sharding import PartitionSpec as P

EPSILON = 1e-05
MESH = pl.DeviceIdType.MESH
BS = 128
CAP = 96
D = 4096
CH = 4
CW = D // CH


def layer(tok_ref, gain_ref, tab_ref, g_hbm, u_hbm, d_hbm, out_ref,
          wg, wu, wd, tabs, tab_s, xz, xf, xa, gate_s, hid_s, sb, rb, sf, gb, rg,
          own, swap, zr, zs, xr, xs, fr, fs, cr, cs, tsem, ssem, gr, gs, yr, ys, yr2, ys2, gr2, gs2):
    t = lax.axis_index("tp")
    d = lax.axis_index("dp")
    hi, y, c = t // 8, (t // 2) % 4, t % 2
    zl, x = d // 4, d % 4
    half, ze = zl // 4, zl % 4
    g = hi * 2 + half

    def dev(hi=hi, y=y, c=c, half=half, ze=ze, x=x):
        return {"tp": hi * 8 + y * 2 + c, "dp": (half * 4 + ze) * 4 + x}

    partner = dev(c=1 - c, half=1 - half)
    zpeer = [None] + [dev(ze=(ze + i) % 4) for i in (1, 2, 3)]
    right, left = dev(x=(x + 1) % 4), dev(x=(x + 3) % 4)
    sib = dev(c=1 - c)
    ypeer = [None] + [dev(y=(y + i) % 4) for i in (1, 2, 3)]
    gpeer = [None]
    for i in (1, 2, 3):
        o = (g + i) % 4
        gpeer.append(dev(hi=o // 2, half=o % 2))

    barrier = pltpu.get_barrier_semaphore()
    peers = [partner, right, left, sib] + zpeer[1:] + ypeer[1:] + gpeer[1:]
    for p in peers:
        pl.semaphore_signal(barrier, inc=1, device_id=p, device_id_type=MESH)
    pl.semaphore_wait(barrier, len(peers))

    W = (wg, wu, wd)
    src = (g_hbm, u_hbm, d_hbm)
    is_home = c == half
    pending = []

    def remote(a, b, s, r, p):
        return pltpu.make_async_remote_copy(
            src_ref=a, dst_ref=b, send_sem=s, recv_sem=r, device_id=p, device_id_type=MESH)

    def piece(q, n, xx):
        p = 16 * c + 4 * ((ze + 4 - n) % 4) + xx % 4
        return W[q].at[pl.ds(p * 3, 3)]

    def swap_copy(q):
        p = 16 * half + 4 * ze + x
        return remote(src[q], W[q].at[pl.ds(p * 3, 3)], swap.at[q], own.at[q], partner)

    def home_copy(q):
        return pltpu.make_async_copy(src[q], piece(q, 0, x), own.at[q])

    @pl.when(is_home)
    def _():
        for q in range(3):
            home_copy(q).start()

    @pl.when(jnp.logical_not(is_home))
    def _():
        for q in range(3):
            swap_copy(q).start()

    tcopy = remote(tab_ref, tabs.at[c], ssem.at[0], tsem.at[0], sib)
    tcopy.start()
    tabs[2] = tab_ref[...]

    v = tok_ref[...].astype(jnp.float32)
    ms = jnp.mean(v * v, axis=-1, keepdims=True)
    xz[g] = (v * lax.rsqrt(ms + EPSILON) * gain_ref[...]).astype(jnp.bfloat16)
    gcopies = [remote(xz.at[g], xz.at[g], gs.at[i], gr.at[i], gpeer[i]) for i in (1, 2, 3)]
    for cp in gcopies:
        cp.start()
    pending.extend(gcopies)

    for q in range(3):
        W[q][CAP] = jnp.zeros((BS, BS), jnp.bfloat16)

    def core_send(q, ref):
        remote(ref, ref, cs.at[q], cr.at[q], sib).start()

    def x_send(q, n):
        ref = piece(q, n, x)
        for k, p in ((0, right), (1, left)):
            cp = remote(ref, ref, xs.at[q, k, n], xr.at[q, k, n], p)
            cp.start()
            pending.append(cp)

    def first(q):
        home_copy(q).wait()
        ref = piece(q, 0, x)
        for i in (2, 1, 3):
            cp = remote(ref, ref, zs.at[q, i], zr.at[q, i], zpeer[i])
            cp.start()
            pending.append(cp)
        x_send(q, 0)
        core_send(q, ref)

    def stage1(q):
        for n in (1, 3, 2):
            ref = piece(q, n, x)
            remote(ref, ref, zs.at[q, n], zr.at[q, n], zpeer[n]).wait_recv()
            x_send(q, n)
            core_send(q, ref)

    def stage2(q):
        for n in (0, 1, 3, 2):
            fl, fright = piece(q, n, x + 3), piece(q, n, x + 1)
            remote(fl, fl, xs.at[q, 0, n], xr.at[q, 0, n], right).wait_recv()
            remote(fright, fright, xs.at[q, 1, n], xr.at[q, 1, n], left).wait_recv()
            ref, p = (fl, right) if n < 2 else (fright, left)
            cp = remote(ref, ref, fs.at[q, n], fr.at[q, n], p)
            cp.start()
            pending.append(cp)
            core_send(q, fl)
            core_send(q, fright)

    def stage3(q):
        for n in (0, 1, 3, 2):
            ref = piece(q, n, x + 2)
            remote(ref, ref, fs.at[q, n], fr.at[q, n], right).wait_recv()
            core_send(q, ref)

    def stage4(q):
        ref = W[q].at[pl.ds(48 * (1 - c), 48)]
        remote(ref, ref, cs.at[q], cr.at[q], sib).wait_recv()

    def w4(q, j, k):
        def one(jj, kk):
            b = jj * 32 + kk
            return W[q][tab_s[2 * q + b // 128, b % 128]]
        return one(j, k), one(j, k + 1), one(j + 1, k), one(j + 1, k + 1)

    def project(q, jp):
        acc = jnp.zeros((64, 256), jnp.float32)
        for kk in range(16):
            a, b, e, f = w4(q, 2 * jp, 2 * kk)
            w = jnp.concatenate(
                [jnp.concatenate([a, e], axis=1), jnp.concatenate([b, f], axis=1)], axis=0)
            xx = xa[:, :, 256 * kk:256 * kk + 256].reshape(64, 256)
            acc = acc + jnp.dot(xx, w, preferred_element_type=jnp.float32)
        return acc

    first(0)
    for i in (1, 2, 3):
        remote(xz.at[(g + 4 - i) % 4], xz.at[(g + 4 - i) % 4], gs.at[i], gr.at[i], gpeer[i]).wait_recv()
    for i in range(4):
        xf[4 * i:4 * i + 4, :] = xz[i].astype(jnp.float32)
    xa[y] = xf[...].astype(jnp.bfloat16)
    ycopies = [remote(xa.at[y], xa.at[y], ys.at[i], yr.at[i], ypeer[i]) for i in (1, 2, 3)]
    for cp in ycopies:
        cp.start()
    pending.extend(ycopies)
    first(1)
    first(2)

    remote(tab_ref, tabs.at[1 - c], ssem.at[0], tsem.at[0], sib).wait_recv()
    mine = pltpu.make_async_copy(tabs.at[jnp.where(is_home, 2, half)], tab_s, tsem.at[1])
    mine.start()
    mine.wait()

    stage1(0)
    stage2(0)
    stage1(1)
    stage3(0)
    stage2(1)
    for i in (1, 2, 3):
        ref = xa.at[(y + 4 - i) % 4]
        remote(ref, ref, ys.at[i], yr.at[i], ypeer[i]).wait_recv()
    stage4(0)

    @pl.loop(0, 4)
    def _(jp):
        gate_s[jp] = project(0, jp)

    stage1(2)
    stage3(1)
    stage2(2)
    stage4(1)

    @pl.loop(0, 4)
    def _(jp):
        up = project(1, jp)
        ga = gate_s[jp]
        hid_s[jp] = (ga / (1.0 + jnp.exp(-ga)) * up).astype(jnp.bfloat16)

    stage3(2)
    stage4(2)

    def y_copy(n, i):
        return remote(sb.at[n, (y + i) % 4], rb.at[n, i], ys2.at[n, i], yr2.at[n, i], ypeer[i])

    def g_copy(n, i):
        return remote(gb.at[n, (g + i) % 4], rg.at[n, i], gs2.at[n, i], gr2.at[n, i], gpeer[i])

    @pl.loop(0, CH)
    def _(n):
        for kp in range(4):
            acc = jnp.zeros((64, 256), jnp.float32)
            for jp in range(4):
                k = n * 8 + 2 * kp
                a, e, b, f = w4(2, 2 * jp, k)
                w = jnp.concatenate(
                    [jnp.concatenate([a, e], axis=1), jnp.concatenate([b, f], axis=1)], axis=0)
                acc = acc + jnp.dot(hid_s[jp], w, preferred_element_type=jnp.float32)
            sb[n, :, :, 256 * kp:256 * kp + 256] = acc.astype(jnp.bfloat16).reshape(4, 16, 256)
        for i in (1, 2, 3):
            y_copy(n, i).start()

    @pl.loop(0, CH)
    def _(n):
        for i in (1, 2, 3):
            y_copy(n, i).wait_recv()
        s = sb[n, y].astype(jnp.float32)
        for i in (1, 2, 3):
            s = s + rb[n, i].astype(jnp.float32)
        sf[...] = s
        for i in range(4):
            gb[n, i] = sf[4 * i:4 * i + 4, :].astype(jnp.bfloat16)
        for i in (1, 2, 3):
            g_copy(n, i).start()

    for n in range(CH):
        for i in (1, 2, 3):
            g_copy(n, i).wait_recv()
        s = gb[n, g].astype(jnp.float32)
        for i in (1, 2, 3):
            s = s + rg[n, i].astype(jnp.float32)
        cols = slice(n * CW, (n + 1) * CW)
        out_ref[:, cols] = (tok_ref[:, cols].astype(jnp.float32) + s).astype(jnp.bfloat16)

    for cp in pending:
        cp.wait_send()
    tcopy.wait_send()
    for q in range(3):
        ref = W[q].at[pl.ds(48 * c, 48)]
        remote(ref, ref, cs.at[q], cr.at[q], sib).wait_send()
    for n in range(CH):
        for i in (1, 2, 3):
            y_copy(n, i).wait_send()
            g_copy(n, i).wait_send()

    @pl.when(jnp.logical_not(is_home))
    def _():
        for q in range(3):
            swap_copy(q).wait_send()


def shards(tokens, norm_gain, gate_slots, up_slots, down_slots, gate_ids, up_ids, down_ids):
    ids = jnp.stack([gate_ids, up_ids, down_ids])
    hit = ids[:, None, :] == jnp.arange(256, dtype=jnp.int32)[None, :, None]
    tab = jnp.min(jnp.where(hit, jnp.arange(CAP, dtype=jnp.int32), CAP), axis=-1)
    tab = jnp.pad(tab.reshape(6, 128), ((0, 2), (0, 0)))
    bf, f32 = jnp.bfloat16, jnp.float32
    dma = pltpu.SemaphoreType.DMA
    vm = pl.BlockSpec(memory_space=pltpu.VMEM)
    hbm = pl.BlockSpec(memory_space=pl.ANY)
    return pl.pallas_call(
        layer,
        out_shape=jax.ShapeDtypeStruct((4, D), bf),
        in_specs=[vm, vm, vm, hbm, hbm, hbm],
        out_specs=vm,
        scratch_shapes=[
            pltpu.VMEM((CAP + 1, BS, BS), bf),
            pltpu.VMEM((CAP + 1, BS, BS), bf),
            pltpu.VMEM((CAP + 1, BS, BS), bf),
            pltpu.VMEM((3, 8, 128), jnp.int32),
            pltpu.SMEM((8, 128), jnp.int32),
            pltpu.VMEM((4, 4, D), bf),
            pltpu.VMEM((16, D), f32),
            pltpu.VMEM((4, 16, D), bf),
            pltpu.VMEM((4, 64, 256), f32),
            pltpu.VMEM((4, 64, 256), bf),
            pltpu.VMEM((CH, 4, 16, CW), bf),
            pltpu.VMEM((CH, 4, 16, CW), bf),
            pltpu.VMEM((16, CW), f32),
            pltpu.VMEM((CH, 4, 4, CW), bf),
            pltpu.VMEM((CH, 4, 4, CW), bf),
            dma((3,)), dma((3,)), dma((3, 4)), dma((3, 4)), dma((3, 2, 4)), dma((3, 2, 4)),
            dma((3, 4)), dma((3, 4)), dma((3,)), dma((3,)), dma((2,)), dma((1,)),
            dma((4,)), dma((4,)), dma((4,)), dma((4,)),
            dma((CH, 4)), dma((CH, 4)), dma((CH, 4)), dma((CH, 4)),
        ],
        compiler_params=pltpu.CompilerParams(
            collective_id=0, has_side_effects=True, vmem_limit_bytes=40 << 20),
    )(tokens, norm_gain.reshape(1, D), tab, gate_slots, up_slots, down_slots)


def solution(mesh):
    placed = (
        P(("tp", "dp"), None),
        P(),
        P(("tp", "dp"), None, None),
        P(("tp", "dp"), None, None),
        P(("tp", "dp"), None, None),
        P("tp"),
        P("tp"),
        P("tp"),
    )
    return jax.shard_map(
        shards, mesh=mesh, in_specs=placed, out_specs=P(("tp", "dp"), None), check_vma=False
    )
```

time: 964 us -> 100 us (0.10)
  the two profiles are of different devices: /device:TPU:1 before, /device:TPU:36 now
where the time goes in v1:
time: 100 us
  Pallas kernels  95.1 us (95%)
  local copies, waits for them, and re-layouts  4.03 us (4%)
    pallas_call x1, Pallas kernels, shards(): pl.pallas_call(layer, out_shape=jax.ShapeDtypeStruct((4, D), bf), in_spec...  95.1 us
    unnamed x11, local copies, waits for them, and re-layouts  4.01 us

profile of v1, /device:TPU:36, one launch (start us, length us, event | category | flops | bytes accessed | tf_op | source)
XLA Modules:
  0.0 100.0 jit_solution(9446181825848922092)
XLA Ops:
  0.0 0.0 copy-start.3
  0.0 0.7 pad_add_fusion
  0.7 0.1 select_reduce_fusion
  0.9 0.0 copy-done.3
  0.9 0.0 copy-start
  0.9 0.9 copy-done
  1.8 0.0 copy-start.1
  1.8 0.9 copy-done.1
  2.7 0.0 copy-start.2
  2.7 0.9 copy-done.2
  3.5 0.0 copy-start.4
  3.6 0.7 copy-done.4
  4.3 95.1 %shard_map.82 = bf16[4,4096]{1,0:T(4,128)(2,1)S(1)} custom-call(bf16[4,4096]{1,0:T(4,128)(2,1)S(1)} %copy-done.3, f32[1,4096]{1,0:T(1,128)S(1)} %bitcast.4, s32[8,128]{1,0:T(8,128)S(1)} %pad.4.tab_ref, bf16[3,128,128]{2,1,0:T(8,128)(2,1)S(1)} %copy-done, bf16[3,128,128]{2,1,0:T(8,128)(2,1)S(1)} %copy-done.1, bf16[3,128,128]{2,1,0:T(8,128)(2,1)S(1)} %copy-done.2), custom_call_target="tpu_custom_call" | custom-call | tf_op jit(solution)/shard_map/pallas_call | solution.py:270
  99.4 0.6 copy.10
  (2 shorter events, 0.0 us)
Async XLA Ops:
  0.0 0.9 copy-start.3
  0.9 0.9 copy-start
  1.8 0.9 copy-start.1
  2.7 0.9 copy-start.2
  3.5 0.7 copy-start.4

commit v2 on v1

--- a/solution.py
+++ b/solution.py
@@ -16,7 +16,7 @@
 
 def layer(tok_ref, gain_ref, tab_ref, g_hbm, u_hbm, d_hbm, out_ref,
           wg, wu, wd, tabs, tab_s, xz, xf, xa, gate_s, hid_s, sb, rb, sf, gb, rg,
-          own, swap, zr, zs, xr, xs, fr, fs, cr, cs, tsem, ssem, gr, gs, yr, ys, yr2, ys2, gr2, gs2):
+          swap, zr, zs, xr, xs, fr, fs, cr, cs, tsem, ssem, gr, gs, yr, ys, yr2, ys2, gr2, gs2):
     t = lax.axis_index("tp")
     d = lax.axis_index("dp")
     hi, y, c = t // 8, (t // 2) % 4, t % 2
@@ -28,7 +28,6 @@
         return {"tp": hi * 8 + y * 2 + c, "dp": (half * 4 + ze) * 4 + x}
 
     partner = dev(c=1 - c, half=1 - half)
-    zpeer = [None] + [dev(ze=(ze + i) % 4) for i in (1, 2, 3)]
     right, left = dev(x=(x + 1) % 4), dev(x=(x + 3) % 4)
     sib = dev(c=1 - c)
     ypeer = [None] + [dev(y=(y + i) % 4) for i in (1, 2, 3)]
@@ -38,11 +37,10 @@
         gpeer.append(dev(hi=o // 2, half=o % 2))
 
     barrier = pltpu.get_barrier_semaphore()
-    peers = [partner, right, left, sib] + zpeer[1:] + ypeer[1:] + gpeer[1:]
+    peers = [partner, right, left, sib] + ypeer[1:] + gpeer[1:] + [
+        dev(ze=(ze + 1) % 4), dev(ze=(ze + 3) % 4)]
     for p in peers:
         pl.semaphore_signal(barrier, inc=1, device_id=p, device_id_type=MESH)
-    pl.semaphore_wait(barrier, len(peers))
-
     W = (wg, wu, wd)
     src = (g_hbm, u_hbm, d_hbm)
     is_home = c == half
@@ -52,22 +50,50 @@
         return pltpu.make_async_remote_copy(
             src_ref=a, dst_ref=b, send_sem=s, recv_sem=r, device_id=p, device_id_type=MESH)
 
-    def piece(q, n, xx):
-        p = 16 * c + 4 * ((ze + 4 - n) % 4) + xx % 4
-        return W[q].at[pl.ds(p * 3, 3)]
+    edge = (ze == 0) | (ze == 3)
+    key = (0, jnp.where(ze == 0, 3, 1), jnp.where(edge, 2, 3),
+           jnp.where(ze == 0, 1, jnp.where(ze == 3, 3, 2)))
+    zpos = [(ze + 4 - k) % 4 for k in key]
+    goes_up = [(ze < 3) & (ze >= k) for k in key]
+    goes_down = [ze > 0] + [(ze > 0) & (ze < k) for k in key[1:]]
+    above = dev(ze=jnp.minimum(ze + 1, 3))
+    below = dev(ze=jnp.maximum(ze - 1, 0))
+
+    def piece(q, m, xx):
+        return W[q].at[pl.ds((16 * c + 4 * zpos[m] + xx % 4) * 3, 3)]
+
+    def z_up(q, m):
+        ref = piece(q, m, x)
+        return remote(ref, ref, zs.at[q, 0, m], zr.at[q, (key[m] + 1) % 4], above)
+
+    def z_down(q, m):
+        ref = piece(q, m, x)
+        return remote(ref, ref, zs.at[q, 1, m], zr.at[q, (key[m] + 3) % 4], below)
 
     def swap_copy(q):
         p = 16 * half + 4 * ze + x
-        return remote(src[q], W[q].at[pl.ds(p * 3, 3)], swap.at[q], own.at[q], partner)
+        return remote(src[q], W[q].at[pl.ds(p * 3, 3)], swap.at[q], zr.at[q, 0], partner)
 
     def home_copy(q):
-        return pltpu.make_async_copy(src[q], piece(q, 0, x), own.at[q])
+        return pltpu.make_async_copy(src[q], piece(q, 0, x), zr.at[q, 0])
 
     @pl.when(is_home)
     def _():
         for q in range(3):
             home_copy(q).start()
 
+    v = tok_ref[...].astype(jnp.float32)
+    ms = jnp.mean(v * v, axis=-1, keepdims=True)
+    xz[g] = (v * lax.rsqrt(ms + EPSILON) * gain_ref[...]).astype(jnp.bfloat16)
+    for q in range(3):
+        W[q][CAP] = jnp.zeros((BS, BS), jnp.bfloat16)
+
+    tabs[2] = tab_ref[...]
+    pl.semaphore_wait(barrier, len(peers))
+
+    gcopies = [remote(xz.at[g], xz.at[g], gs.at[i], gr.at[i], gpeer[i]) for i in (1, 2, 3)]
+    pending.extend(gcopies)
+
     @pl.when(jnp.logical_not(is_home))
     def _():
         for q in range(3):
@@ -75,63 +101,49 @@
 
     tcopy = remote(tab_ref, tabs.at[c], ssem.at[0], tsem.at[0], sib)
     tcopy.start()
-    tabs[2] = tab_ref[...]
-
-    v = tok_ref[...].astype(jnp.float32)
-    ms = jnp.mean(v * v, axis=-1, keepdims=True)
-    xz[g] = (v * lax.rsqrt(ms + EPSILON) * gain_ref[...]).astype(jnp.bfloat16)
-    gcopies = [remote(xz.at[g], xz.at[g], gs.at[i], gr.at[i], gpeer[i]) for i in (1, 2, 3)]
-    for cp in gcopies:
-        cp.start()
-    pending.extend(gcopies)
-
-    for q in range(3):
-        W[q][CAP] = jnp.zeros((BS, BS), jnp.bfloat16)
 
     def core_send(q, ref):
         remote(ref, ref, cs.at[q], cr.at[q], sib).start()
 
-    def x_send(q, n):
-        ref = piece(q, n, x)
-        for k, p in ((0, right), (1, left)):
-            cp = remote(ref, ref, xs.at[q, k, n], xr.at[q, k, n], p)
-            cp.start()
-            pending.append(cp)
-
-    def first(q):
-        home_copy(q).wait()
-        ref = piece(q, 0, x)
-        for i in (2, 1, 3):
-            cp = remote(ref, ref, zs.at[q, i], zr.at[q, i], zpeer[i])
-            cp.start()
-            pending.append(cp)
-        x_send(q, 0)
+    def x_copy(q, k, m):
+        ref = piece(q, m, x)
+        return remote(ref, ref, xs.at[q, k, m], xr.at[q, k, m], left if k else right)
+
+    def f_copy(q, m):
+        ref, p = (piece(q, m, x + 1), left) if m % 2 else (piece(q, m, x + 3), right)
+        return remote(ref, ref, fs.at[q, m], fr.at[q, m], p)
+
+    def x_send(q, m):
+        x_copy(q, 0, m).start()
+        x_copy(q, 1, m).start()
+
+    def step(q, m):
+        ref = piece(q, m, x)
+        remote(ref, ref, zs.at[q, 0, m], zr.at[q, key[m]], above).wait_recv()
+
+        @pl.when(goes_up[m])
+        def _():
+            z_up(q, m).start()
+
+        @pl.when(goes_down[m])
+        def _():
+            z_down(q, m).start()
+
+        x_send(q, m)
         core_send(q, ref)
 
-    def stage1(q):
-        for n in (1, 3, 2):
-            ref = piece(q, n, x)
-            remote(ref, ref, zs.at[q, n], zr.at[q, n], zpeer[n]).wait_recv()
-            x_send(q, n)
-            core_send(q, ref)
-
-    def stage2(q):
-        for n in (0, 1, 3, 2):
-            fl, fright = piece(q, n, x + 3), piece(q, n, x + 1)
-            remote(fl, fl, xs.at[q, 0, n], xr.at[q, 0, n], right).wait_recv()
-            remote(fright, fright, xs.at[q, 1, n], xr.at[q, 1, n], left).wait_recv()
-            ref, p = (fl, right) if n < 2 else (fright, left)
-            cp = remote(ref, ref, fs.at[q, n], fr.at[q, n], p)
-            cp.start()
-            pending.append(cp)
-            core_send(q, fl)
-            core_send(q, fright)
-
-    def stage3(q):
-        for n in (0, 1, 3, 2):
-            ref = piece(q, n, x + 2)
-            remote(ref, ref, fs.at[q, n], fr.at[q, n], right).wait_recv()
-            core_send(q, ref)
+    def forward(q, m):
+        fl, fright = piece(q, m, x + 3), piece(q, m, x + 1)
+        remote(fl, fl, xs.at[q, 0, m], xr.at[q, 0, m], right).wait_recv()
+        remote(fright, fright, xs.at[q, 1, m], xr.at[q, 1, m], left).wait_recv()
+        f_copy(q, m).start()
+        core_send(q, fl)
+        core_send(q, fright)
+
+    def far(q, m):
+        ref = piece(q, m, x + 2)
+        remote(ref, ref, fs.at[q, m], fr.at[q, m], right).wait_recv()
+        core_send(q, ref)
 
     def stage4(q):
         ref = W[q].at[pl.ds(48 * (1 - c), 48)]
@@ -153,41 +165,65 @@
             acc = acc + jnp.dot(xx, w, preferred_element_type=jnp.float32)
         return acc
 
-    first(0)
-    for i in (1, 2, 3):
-        remote(xz.at[(g + 4 - i) % 4], xz.at[(g + 4 - i) % 4], gs.at[i], gr.at[i], gpeer[i]).wait_recv()
-    for i in range(4):
-        xf[4 * i:4 * i + 4, :] = xz[i].astype(jnp.float32)
-    xa[y] = xf[...].astype(jnp.bfloat16)
-    ycopies = [remote(xa.at[y], xa.at[y], ys.at[i], yr.at[i], ypeer[i]) for i in (1, 2, 3)]
-    for cp in ycopies:
-        cp.start()
-    pending.extend(ycopies)
-    first(1)
-    first(2)
-
-    remote(tab_ref, tabs.at[1 - c], ssem.at[0], tsem.at[0], sib).wait_recv()
-    mine = pltpu.make_async_copy(tabs.at[jnp.where(is_home, 2, half)], tab_s, tsem.at[1])
-    mine.start()
-    mine.wait()
-
-    stage1(0)
-    stage2(0)
-    stage1(1)
-    stage3(0)
-    stage2(1)
-    for i in (1, 2, 3):
-        ref = xa.at[(y + 4 - i) % 4]
-        remote(ref, ref, ys.at[i], yr.at[i], ypeer[i]).wait_recv()
+    def tokens_g():
+        for i in (1, 2, 3):
+            ref = xz.at[(g + 4 - i) % 4]
+            remote(ref, ref, gs.at[i], gr.at[i], gpeer[i]).wait_recv()
+        for i in range(4):
+            xf[4 * i:4 * i + 4, :] = xz[i].astype(jnp.float32)
+        xa[y] = xf[...].astype(jnp.bfloat16)
+        for i in (1, 2, 3):
+            cp = remote(xa.at[y], xa.at[y], ys.at[i], yr.at[i], ypeer[i])
+            cp.start()
+            pending.append(cp)
+
+    def tokens_y():
+        for i in (1, 2, 3):
+            ref = xa.at[(y + 4 - i) % 4]
+            remote(ref, ref, ys.at[i], yr.at[i], ypeer[i]).wait_recv()
+        remote(tab_ref, tabs.at[1 - c], ssem.at[0], tsem.at[0], sib).wait_recv()
+        mine = pltpu.make_async_copy(tabs.at[jnp.where(is_home, 2, half)], tab_s, tsem.at[1])
+        mine.start()
+        mine.wait()
+
+    items = [(q, m) for q in range(3) for m in range(4)]
+
+    @pl.when(is_home)
+    def _():
+        for q in range(3):
+            step(q, 0)
+
+    for p in range(12):
+        q, m = items[p]
+        if m == 0:
+            @pl.when(jnp.logical_not(is_home))
+            def _():
+                step(q, 0)
+        else:
+            step(q, m)
+        if p >= 4:
+            forward(*items[p - 4])
+        if p >= 8:
+            far(*items[p - 8])
+        if p == 6:
+            for cp in gcopies:
+                cp.start()
+    forward(*items[8])
+    tokens_g()
+    forward(*items[9])
+    forward(*items[10])
+    forward(*items[11])
+    for p in (4, 5):
+        far(*items[p])
+    tokens_y()
     stage4(0)
 
     @pl.loop(0, 4)
     def _(jp):
         gate_s[jp] = project(0, jp)
 
-    stage1(2)
-    stage3(1)
-    stage2(2)
+    for p in (6, 7, 8, 9):
+        far(*items[p])
     stage4(1)
 
     @pl.loop(0, 4)
@@ -196,7 +232,8 @@
         ga = gate_s[jp]
         hid_s[jp] = (ga / (1.0 + jnp.exp(-ga)) * up).astype(jnp.bfloat16)
 
-    stage3(2)
+    for p in (10, 11):
+        far(*items[p])
     stage4(2)
 
     def y_copy(n, i):
@@ -245,6 +282,20 @@
         cp.wait_send()
     tcopy.wait_send()
     for q in range(3):
+        for m in range(4):
+            x_copy(q, 0, m).wait_send()
+            x_copy(q, 1, m).wait_send()
+            f_copy(q, m).wait_send()
+        for m in range(4):
+            @pl.when(goes_up[m])
+            def _():
+                z_up(q, m).wait_send()
+
+            @pl.when(goes_down[m])
+            def _():
+                z_down(q, m).wait_send()
+
+    for q in range(3):
         ref = W[q].at[pl.ds(48 * c, 48)]
         remote(ref, ref, cs.at[q], cr.at[q], sib).wait_send()
     for n in range(CH):
@@ -266,7 +317,7 @@
     bf, f32 = jnp.bfloat16, jnp.float32
     dma = pltpu.SemaphoreType.DMA
     vm = pl.BlockSpec(memory_space=pltpu.VMEM)
-    hbm = pl.BlockSpec(memory_space=pl.ANY)
+    hbm = pl.BlockSpec(memory_space=pltpu.MemorySpace.HBM)
     return pl.pallas_call(
         layer,
         out_shape=jax.ShapeDtypeStruct((4, D), bf),
@@ -288,13 +339,13 @@
             pltpu.VMEM((16, CW), f32),
             pltpu.VMEM((CH, 4, 4, CW), bf),
             pltpu.VMEM((CH, 4, 4, CW), bf),
-            dma((3,)), dma((3,)), dma((3, 4)), dma((3, 4)), dma((3, 2, 4)), dma((3, 2, 4)),
+            dma((3,)), dma((3, 4)), dma((3, 2, 4)), dma((3, 2, 4)), dma((3, 2, 4)),
             dma((3, 4)), dma((3, 4)), dma((3,)), dma((3,)), dma((2,)), dma((1,)),
             dma((4,)), dma((4,)), dma((4,)), dma((4,)),
             dma((CH, 4)), dma((CH, 4)), dma((CH, 4)), dma((CH, 4)),
         ],
         compiler_params=pltpu.CompilerParams(
-            collective_id=0, has_side_effects=True, vmem_limit_bytes=40 << 20),
+            collective_id=0, has_side_effects=True, vmem_limit_bytes=63 << 20),
     )(tokens, norm_gain.reshape(1, D), tab, gate_slots, up_slots, down_slots)
 
 

time: 100 us -> 96.3 us (0.963)
  the two profiles are of different devices: /device:TPU:36 before, /device:TPU:6 now
where the time goes in v2:
time: 96.3 us; the launch traced here: 96 us
  Pallas kernels  93.2 us (97%)
  local copies, waits for them, and re-layouts  2.68 us (3%)
    pallas_call x1, Pallas kernels, shards(): pl.pallas_call(layer, out_shape=jax.ShapeDtypeStruct((4, D), bf), in_spec...  93.2 us
    unnamed x7, local copies, waits for them, and re-layouts  2.07 us

profile of v2, /device:TPU:6, one launch (start us, length us, event | category | flops | bytes accessed | tf_op | source)
XLA Modules:
  0.0 96.0 jit_solution(9170467376176004482)
XLA Ops:
  0.0 0.0 copy-start
  0.0 0.0 copy-start.1
  0.0 0.0 copy-start.2
  0.0 0.6 copy-done
  0.7 0.0 copy-done.1
  0.7 0.0 copy-done.2
  0.7 0.1 select_reduce_fusion
  0.8 0.6 pad.4.tab_ref
  1.4 93.2 %shard_map.82 = bf16[4,4096]{1,0:T(4,128)(2,1)} custom-call(bf16[4,4096]{1,0:T(4,128)(2,1)} %tok_ref.1, f32[1,4096]{1,0:T(1,128)} %bitcast.4, s32[8,128]{1,0:T(8,128)} %pad.4.tab_ref, bf16[3,128,128]{2,1,0:T(8,128)(2,1)} %g_hbm.1, bf16[3,128,128]{2,1,0:T(8,128)(2,1)} %u_hbm.1, bf16[3,128,128]{2,1,0:T(8,128)(2,1)} %d_hbm.1), custom_call_target="tpu_custom_call" | custom-call | tf_op jit(solution)/shard_map/pallas_call | solution.py:321
  94.6 1.4 %copy.10 = bf16[4,4096]{1,0:T(4,128)(2,1)} copy(bf16[4,4096]{1,0:T(4,128)(2,1)} %shard_map.82) | data formatting | bytes 65536
  (2 shorter events, 0.0 us)
Async XLA Ops:
  0.0 0.7 copy-start
  0.0 0.7 copy-start.1
  0.0 0.7 copy-start.2

commit v3 on v2

--- a/solution.py
+++ b/solution.py
@@ -15,8 +15,8 @@
 
 
 def layer(tok_ref, gain_ref, tab_ref, g_hbm, u_hbm, d_hbm, out_ref,
-          wg, wu, wd, tabs, tab_s, xz, xf, xa, gate_s, hid_s, sb, rb, sf, gb, rg,
-          swap, zr, zs, xr, xs, fr, fs, cr, cs, tsem, ssem, gr, gs, yr, ys, yr2, ys2, gr2, gs2):
+          wg, wu, wd, tabs, tab_s, xz, xf, xa, gate_s, hid_s, sb, rb, sf, gb, rg, stage,
+          swap, staged, zr, zs, xr, xs, fr, fs, cr, cs, tsem, ssem, gr, gs, yr, ys, yr2, ys2, gr2, gs2):
     t = lax.axis_index("tp")
     d = lax.axis_index("dp")
     hi, y, c = t // 8, (t // 2) % 4, t % 2
@@ -27,7 +27,8 @@
     def dev(hi=hi, y=y, c=c, half=half, ze=ze, x=x):
         return {"tp": hi * 8 + y * 2 + c, "dp": (half * 4 + ze) * 4 + x}
 
-    partner = dev(c=1 - c, half=1 - half)
+    entry = dev(c=1 - c, half=1 - half, ze=3 * half)
+    across = [dev(c=1 - c, half=1 - half, ze=i) for i in range(4)]
     right, left = dev(x=(x + 1) % 4), dev(x=(x + 3) % 4)
     sib = dev(c=1 - c)
     ypeer = [None] + [dev(y=(y + i) % 4) for i in (1, 2, 3)]
@@ -37,7 +38,7 @@
         gpeer.append(dev(hi=o // 2, half=o % 2))
 
     barrier = pltpu.get_barrier_semaphore()
-    peers = [partner, right, left, sib] + ypeer[1:] + gpeer[1:] + [
+    peers = across + [right, left, sib] + ypeer[1:] + gpeer[1:] + [
         dev(ze=(ze + 1) % 4), dev(ze=(ze + 3) % 4)]
     for p in peers:
         pl.semaphore_signal(barrier, inc=1, device_id=p, device_id_type=MESH)
@@ -51,11 +52,12 @@
             src_ref=a, dst_ref=b, send_sem=s, recv_sem=r, device_id=p, device_id_type=MESH)
 
     edge = (ze == 0) | (ze == 3)
-    key = (0, jnp.where(ze == 0, 3, 1), jnp.where(edge, 2, 3),
-           jnp.where(ze == 0, 1, jnp.where(ze == 3, 3, 2)))
-    zpos = [(ze + 4 - k) % 4 for k in key]
-    goes_up = [(ze < 3) & (ze >= k) for k in key]
-    goes_down = [ze > 0] + [(ze > 0) & (ze < k) for k in key[1:]]
+    order = (0, jnp.where(ze == 0, 3, 1), jnp.where(edge, 2, 3),
+             jnp.where(ze == 0, 1, jnp.where(ze == 3, 3, 2)))
+    zpos = [jnp.where(is_home, (ze + 4 - order[m]) % 4, jnp.where(half == 0, m, 3 - m)) for m in range(4)]
+    key = [jnp.where(is_home, order[m], m) for m in range(4)]
+    goes_up = [(ze < 3) & jnp.where(is_home, ze >= order[m], half == 1) for m in range(4)]
+    goes_down = [(ze > 0) & jnp.where(is_home, (ze < order[m]) | (m == 0), half == 0) for m in range(4)]
     above = dev(ze=jnp.minimum(ze + 1, 3))
     below = dev(ze=jnp.maximum(ze - 1, 0))
 
@@ -64,15 +66,16 @@
 
     def z_up(q, m):
         ref = piece(q, m, x)
-        return remote(ref, ref, zs.at[q, 0, m], zr.at[q, (key[m] + 1) % 4], above)
+        return remote(ref, ref, zs.at[q, 0, m], zr.at[q, jnp.where(is_home, (order[m] + 1) % 4, m)], above)
 
     def z_down(q, m):
         ref = piece(q, m, x)
-        return remote(ref, ref, zs.at[q, 1, m], zr.at[q, (key[m] + 3) % 4], below)
+        return remote(ref, ref, zs.at[q, 1, m], zr.at[q, jnp.where(is_home, (order[m] + 3) % 4, m)], below)
 
     def swap_copy(q):
         p = 16 * half + 4 * ze + x
-        return remote(src[q], W[q].at[pl.ds(p * 3, 3)], swap.at[q], zr.at[q, 0], partner)
+        m = jnp.where(half == 1, ze, 3 - ze)
+        return remote(stage.at[q], W[q].at[pl.ds(p * 3, 3)], swap.at[q], zr.at[q, m], entry)
 
     def home_copy(q):
         return pltpu.make_async_copy(src[q], piece(q, 0, x), zr.at[q, 0])
@@ -81,6 +84,14 @@
     def _():
         for q in range(3):
             home_copy(q).start()
+
+    def stage_copy(q):
+        return pltpu.make_async_copy(src[q], stage.at[q], staged.at[q])
+
+    @pl.when(jnp.logical_not(is_home))
+    def _():
+        for q in range(3):
+            stage_copy(q).start()
 
     v = tok_ref[...].astype(jnp.float32)
     ms = jnp.mean(v * v, axis=-1, keepdims=True)
@@ -97,6 +108,7 @@
     @pl.when(jnp.logical_not(is_home))
     def _():
         for q in range(3):
+            stage_copy(q).wait()
             swap_copy(q).start()
 
     tcopy = remote(tab_ref, tabs.at[c], ssem.at[0], tsem.at[0], sib)
@@ -193,47 +205,59 @@
         for q in range(3):
             step(q, 0)
 
-    for p in range(12):
-        q, m = items[p]
-        if m == 0:
-            @pl.when(jnp.logical_not(is_home))
-            def _():
-                step(q, 0)
-        else:
-            step(q, m)
-        if p >= 4:
-            forward(*items[p - 4])
-        if p >= 8:
-            far(*items[p - 8])
-        if p == 6:
-            for cp in gcopies:
-                cp.start()
+    def other_step(p):
+        @pl.when(jnp.logical_not(is_home))
+        def _():
+            step(*items[p])
+
+    other_step(0)
+    step(*items[1])
+    step(*items[2])
+    step(*items[3])
+    other_step(4)
+    forward(*items[0])
+    step(*items[5])
+    forward(*items[1])
+    step(*items[6])
+    forward(*items[2])
+    for cp in gcopies:
+        cp.start()
+    step(*items[7])
+    forward(*items[3])
+    other_step(8)
+    forward(*items[4])
+    far(*items[0])
+    step(*items[9])
+    forward(*items[5])
+    far(*items[1])
+    step(*items[10])
+    forward(*items[6])
+    far(*items[2])
+    step(*items[11])
+    forward(*items[7])
+    far(*items[3])
     forward(*items[8])
+    far(*items[4])
     tokens_g()
     forward(*items[9])
+    far(*items[5])
     forward(*items[10])
+    far(*items[6])
+    tokens_y()
     forward(*items[11])
-    for p in (4, 5):
-        far(*items[p])
-    tokens_y()
     stage4(0)
-
-    @pl.loop(0, 4)
-    def _(jp):
+    for jp in range(4):
         gate_s[jp] = project(0, jp)
-
-    for p in (6, 7, 8, 9):
-        far(*items[p])
+    far(*items[7])
     stage4(1)
-
-    @pl.loop(0, 4)
-    def _(jp):
+    for jp in range(4):
         up = project(1, jp)
         ga = gate_s[jp]
         hid_s[jp] = (ga / (1.0 + jnp.exp(-ga)) * up).astype(jnp.bfloat16)
-
-    for p in (10, 11):
-        far(*items[p])
+    far(*items[8])
+    far(*items[9])
+    far(*items[10])
+    far(*items[11])
     stage4(2)
 
     def y_copy(n, i):
@@ -242,8 +266,7 @@
     def g_copy(n, i):
         return remote(gb.at[n, (g + i) % 4], rg.at[n, i], gs2.at[n, i], gr2.at[n, i], gpeer[i])
 
-    @pl.loop(0, CH)
-    def _(n):
+    for n in range(CH):
         for kp in range(4):
             acc = jnp.zeros((64, 256), jnp.float32)
             for jp in range(4):
@@ -256,8 +279,7 @@
         for i in (1, 2, 3):
             y_copy(n, i).start()
 
-    @pl.loop(0, CH)
-    def _(n):
+    for n in range(CH):
         for i in (1, 2, 3):
             y_copy(n, i).wait_recv()
         s = sb[n, y].astype(jnp.float32)
@@ -339,7 +361,8 @@
             pltpu.VMEM((16, CW), f32),
             pltpu.VMEM((CH, 4, 4, CW), bf),
             pltpu.VMEM((CH, 4, 4, CW), bf),
-            dma((3,)), dma((3, 4)), dma((3, 2, 4)), dma((3, 2, 4)), dma((3, 2, 4)),
+            pltpu.VMEM((3, 3, BS, BS), bf),
+            dma((3,)), dma((3,)), dma((3, 4)), dma((3, 2, 4)), dma((3, 2, 4)), dma((3, 2, 4)),
             dma((3, 4)), dma((3, 4)), dma((3,)), dma((3,)), dma((2,)), dma((1,)),
             dma((4,)), dma((4,)), dma((4,)), dma((4,)),
             dma((CH, 4)), dma((CH, 4)), dma((CH, 4)), dma((CH, 4)),

time: 96.3 us -> 92.3 us (0.958)
  the two profiles are of different devices: /device:TPU:6 before, /device:TPU:1 now
where the time goes in v3:
time: 92.3 us; the launch traced here: 92.1 us
  Pallas kernels  89.2 us (97%)
  local copies, waits for them, and re-layouts  2.68 us (3%)
    pallas_call x1, Pallas kernels, shards(): pl.pallas_call(layer, out_shape=jax.ShapeDtypeStruct((4, D), bf), in_spec...  89.2 us
    unnamed x7, local copies, waits for them, and re-layouts  2.07 us

profile of v3, /device:TPU:1, one launch (start us, length us, event | category | flops | bytes accessed | tf_op | source)
XLA Modules:
  0.0 92.1 jit_solution(3715911014991326398)
XLA Ops:
  0.0 0.0 copy-start
  0.0 0.0 copy-start.1
  0.0 0.0 copy-start.2
  0.0 0.6 copy-done
  0.7 0.0 copy-done.1
  0.7 0.0 copy-done.2
  0.7 0.1 select_reduce_fusion
  0.8 0.6 pad.4.tab_ref
  1.4 89.2 %shard_map.82 = bf16[4,4096]{1,0:T(4,128)(2,1)} custom-call(bf16[4,4096]{1,0:T(4,128)(2,1)} %tok_ref.1, f32[1,4096]{1,0:T(1,128)} %bitcast.4, s32[8,128]{1,0:T(8,128)} %pad.4.tab_ref, bf16[3,128,128]{2,1,0:T(8,128)(2,1)} %g_hbm.1, bf16[3,128,128]{2,1,0:T(8,128)(2,1)} %u_hbm.1, bf16[3,128,128]{2,1,0:T(8,128)(2,1)} %d_hbm.1), custom_call_target="tpu_custom_call" | custom-call | tf_op jit(solution)/shard_map/pallas_call | solution.py:343
  90.7 1.4 %copy.10 = bf16[4,4096]{1,0:T(4,128)(2,1)} copy(bf16[4,4096]{1,0:T(4,128)(2,1)} %shard_map.82) | data formatting | bytes 65536
  (2 shorter events, 0.0 us)
Async XLA Ops:
  0.0 0.7 copy-start
  0.0 0.7 copy-start.1
  0.0 0.7 copy-start.2

commit v4 on v3

--- a/solution.py
+++ b/solution.py
@@ -109,6 +109,7 @@
     def _():
         for q in range(3):
             stage_copy(q).wait()
+        for q in range(1):
             swap_copy(q).start()
 
     tcopy = remote(tab_ref, tabs.at[c], ssem.at[0], tsem.at[0], sib)
@@ -205,14 +206,26 @@
         for q in range(3):
             step(q, 0)
 
+    def later_swap(q):
+        @pl.when(jnp.logical_not(is_home))
+        def _():
+            swap_copy(q).start()
+
+    def later_home(q):
+        @pl.when(is_home)
+        def _():
+            step(q, 0)
+
     def other_step(p):
         @pl.when(jnp.logical_not(is_home))
         def _():
             step(*items[p])
 
     other_step(0)
+    later_swap(1)
     step(*items[1])
     step(*items[2])
+    later_swap(2)
     step(*items[3])
     other_step(4)
     forward(*items[0])

time: 92.3 us -> 90.4 us (0.979)
  Pallas kernels: 89.2 us -> 87.3 us
    pallas_call x1, Pallas kernels: 89.2 us -> 87.3 us  [shards(): pl.pallas_call(layer, out_shape=jax.ShapeDtypeStruct((4, D), bf), in_spec...]
where the time goes in v4:
time: 90.4 us; the launch traced here: 90.1 us
  Pallas kernels  87.3 us (97%)
  local copies, waits for them, and re-layouts  2.68 us (3%)
    pallas_call x1, Pallas kernels, shards(): pl.pallas_call(layer, out_shape=jax.ShapeDtypeStruct((4, D), bf), in_spec...  87.3 us
    unnamed x7, local copies, waits for them, and re-layouts  2.07 us

profile of v4, /device:TPU:1, one launch (start us, length us, event | category | flops | bytes accessed | tf_op | source)
XLA Modules:
  0.0 90.1 jit_solution(683804570689115299)
XLA Ops:
  0.0 0.0 copy-start
  0.0 0.0 copy-start.1
  0.0 0.0 copy-start.2
  0.0 0.6 copy-done
  0.7 0.0 copy-done.1
  0.7 0.0 copy-done.2
  0.7 0.1 select_reduce_fusion
  0.8 0.6 pad.4.tab_ref
  1.4 87.3 %shard_map.82 = bf16[4,4096]{1,0:T(4,128)(2,1)} custom-call(bf16[4,4096]{1,0:T(4,128)(2,1)} %tok_ref.1, f32[1,4096]{1,0:T(1,128)} %bitcast.4, s32[8,128]{1,0:T(8,128)} %pad.4.tab_ref, bf16[3,128,128]{2,1,0:T(8,128)(2,1)} %g_hbm.1, bf16[3,128,128]{2,1,0:T(8,128)(2,1)} %u_hbm.1, bf16[3,128,128]{2,1,0:T(8,128)(2,1)} %d_hbm.1), custom_call_target="tpu_custom_call" | custom-call | tf_op jit(solution)/shard_map/pallas_call | solution.py:356
  88.7 1.4 %copy.10 = bf16[4,4096]{1,0:T(4,128)(2,1)} copy(bf16[4,4096]{1,0:T(4,128)(2,1)} %shard_map.82) | data formatting | bytes 65536
  (2 shorter events, 0.0 us)
Async XLA Ops:
  0.0 0.7 copy-start
  0.0 0.7 copy-start.1
  0.0 0.7 copy-start.2
